TPU v7x, 32 devices: a whole 2x2x4 slice. The times are simulated.
32 devices in a mesh: groups: 2 (over y), strip: 8 (over z, x), chan: 2 (over core).
Axes of the slice: x: 2, y: 2, z: 4, core: 2. Of those that a mesh axis runs over, the one named last changes fastest.
Arguments:
- sky_cube: bfloat16 [32, 512, 1024], P('chan', 'strip', 'groups'), parts along dimension 2, may hold values from -80 to 80
- chan_flags: int32 [32], P('chan'), may hold values 0 or 1
Outputs:
- snr_peak: bfloat16 [32, 512, 1024], P('chan', 'strip', 'groups'), parts along dimension 2
There are 2 independent parts, one for each index of `groups`. A program takes and returns all parts, laid end to end along the dimension named above; an argument that names none is the same for every part. Nothing has to cross between parts.
All inputs are finite; a program needn't handle non-finite values. No bound on the sum of `chan_flags` on one device may be relied on, other than what follows from the above.
Results may differ from a plain program's by a relative error of at most 0.0054.
Values may be sent and summed in bfloat16 or wider, within the bound.
No kernel may reach another device: no remote copies, remote signals or barrier semaphores. Data moves between devices by JAX's collectives and lax.ppermute only.
A program may use at most 64 MiB of HBM per device.

v0:
```python
import functools
import math

import jax
import jax.numpy as jnp
import numpy as np
from jax import lax
from jax.experimental import pallas as pl
from jax.experimental.pallas import tpu as pltpu
from jax.sharding import PartitionSpec as P

gauss_settings = ((5.0, 8), (10.0, 15))
epsilon = 1e-06
clip_level = 3.0
RIM = 3
REACH = 15
EDGE = 16
LANES = 128
BLOCK = 2 * LANES
VMEM, HBM, SMEM = pltpu.VMEM, pltpu.HBM, pltpu.SMEM
f32, bf16 = jnp.float32, jnp.bfloat16


def gauss_weights(fwhm, radius):
    offsets = np.arange(-REACH, REACH + 1)
    spread = fwhm / (2.0 * math.sqrt(2.0 * math.log(2.0)))
    weights = np.exp(-(offsets**2) / (2.0 * spread**2)) * (np.abs(offsets) <= radius)
    weights = weights / weights.sum()
    return weights.astype(np.float32)


def band(out_positions, in_positions):
    offset = np.asarray(in_positions)[None, :] - np.asarray(out_positions)[:, None]
    inside = np.abs(offset) <= REACH
    index = np.clip(offset + REACH, 0, 2 * REACH)
    return np.stack([np.where(inside, gauss_weights(*s)[index], 0.0) for s in gauss_settings])


def constant(matrix):
    return jnp.asarray(matrix.astype(np.float32)).astype(bf16)


def fold(values):
    rows, cols = values.shape
    total = None
    for r in range(0, rows, 8):
        for c in range(0, cols, LANES):
            part = values[r : r + 8, c : c + LANES]
            total = part if total is None else total + part
    return total


def wide(ref, row, rows=EDGE):
    return jnp.broadcast_to(ref[pl.ds(row, 1), :], (rows, LANES))


def towards(chan_count, turns):
    last = chan_count - RIM
    if turns == 1:
        return [jnp.where(lax.axis_index("chan") == 0, last, 0)]
    return [last, 0]


def rest(chan_count, turns):
    if turns == 1:
        return jnp.where(lax.axis_index("chan") == 0, 0, RIM), chan_count - RIM
    return RIM, chan_count - 2 * RIM


def pair_rows(n_rows, pair):
    odd = lax.rem(lax.axis_index("strip"), 2)
    at_end = odd == pair
    return pl.multiple_of(jnp.where(at_end, n_rows - EDGE, 0), EDGE)


def spectral_slot(chan_count, w, c):
    return w * chan_count + c


def smooth_slot(chan_count, w, f, c):
    return (2 + 2 * w + f) * chan_count + c


def means(x):
    for i in range(RIM, len(x) - RIM):
        s3 = x[i - 1] + x[i] + x[i + 1]
        s7 = (x[i - 3] + x[i - 2]) + s3 + (x[i + 2] + x[i + 3])
        yield i - RIM, [(s3 * (1.0 / 3.0)).astype(bf16), (s7 * (1.0 / 7.0)).astype(bf16)]


def row_pass(taps, plane, rowwise, slots, count, at=0):
    per = taps.shape[0] // 2
    for i in range(count):
        row = jnp.dot(taps, plane(slots[i]), preferred_element_type=f32).astype(bf16)
        start = (at + i) * per
        if not isinstance(start, int):
            start = pl.multiple_of(start, per)
        for f in range(2):
            rowwise[f, pl.ds(start, per), :] = row[f * per : (f + 1) * per]


def column_pass(rowwise, matrix, count, put):
    n_cols = rowwise.shape[2]
    per = rowwise.shape[1] // count
    blocks = n_cols // BLOCK
    for f in range(2):
        products = []
        for i in range(2 * blocks - 1):
            b = i * BLOCK if i < blocks else (i - blocks) * BLOCK + LANES
            x = rowwise[f, :, b : b + BLOCK]
            products.append(jnp.dot(x, matrix[f, i], preferred_element_type=f32))
        diagonal, seams = products[:blocks], products[blocks:]
        for slot in range(count):
            rows = slice(slot * per, (slot + 1) * per)
            values = []
            for l in range(0, n_cols, LANES):
                b, right = l // BLOCK, l % BLOCK
                value = diagonal[b][rows, right : right + LANES]
                if right and b < len(seams):
                    value = value + seams[b][rows, :LANES]
                if not right and b > 0:
                    value = value + seams[b - 1][rows, LANES:]
                values.append(value)
            put(f, slot, values)


def put_tiles(smooth, squares, acc, f, start, slot, values, add=False):
    rows = pl.ds(start, values[0].shape[0])
    total = None
    for i, value in enumerate(values):
        cols = slice(i * LANES, (i + 1) * LANES)
        square = value * value
        smooth[f, rows, cols] = value
        squares[f, rows, cols] = square
        part = fold(square)
        total = part if total is None else total + part
    acc[slot] = acc[slot] + total if add else total


def run(copies):
    for copy in copies:
        copy.start()
    for copy in copies:
        copy.wait()


def packed(chan_count):
    return chan_count - 1 if chan_count > REACH else chan_count


def spare_row(at_end):
    tile = pl.ds(pl.multiple_of(jnp.where(at_end, 0, EDGE - 8), 8), 8)
    return tile, jnp.where(at_end, 0, 7), jnp.where(at_end, 1, 0)


def pick_kernel(sky, first_pair, second_pair, last, lasts, sems):
    chan_count, n_rows, n_cols = sky.shape
    sent = packed(chan_count)
    pieces = (first_pair, second_pair)
    starts = [pair_rows(n_rows, pair) for pair in range(2)]
    copies = []
    for pair in range(2):
        rows = pl.ds(starts[pair], EDGE)
        source = sky.at[:sent, rows, :]
        copies.append(pltpu.make_async_copy(source, pieces[pair], sems.at[2 * pair]))
        if sent < chan_count:
            source = sky.at[sent, rows, :]
            copies.append(pltpu.make_async_copy(source, last.at[pair], sems.at[2 * pair + 1]))
    run(copies)
    if sent == chan_count:
        return
    row_index = lax.broadcasted_iota(jnp.int32, (8, n_cols), 0)
    for pair in range(2):
        tile, spare, first = spare_row(starts[pair] > 0)
        lasts[pair] = last[pair].astype(f32)
        for i in range(REACH):
            row = jnp.broadcast_to(lasts[pair, pl.ds(first + i, 1), :], (8, n_cols))
            value = pieces[pair][i, tile, :].astype(f32)
            value = jnp.where(row_index == spare, row, value)
            pieces[pair][i, tile, :] = value.astype(bf16)


def unpack(pair, n_rows, halo, last):
    tile, _, first = spare_row(pair_rows(n_rows, pair) == 0)
    last[...] = jnp.zeros_like(last)
    for i in range(REACH):
        value = halo[i, tile, :].astype(f32)
        last[pl.ds(first + i, 1), :] = jnp.where(first == 1, value[:1], value[7:])


def halo_tile(halo, last, c, cols, may_be_last):
    value = halo[jnp.clip(c, 0, halo.shape[0] - 1), :, cols].astype(f32)
    if may_be_last:
        value = jnp.where(c == halo.shape[0], last[:, cols], value)
    return value


def rim_kernel(flags, sky, rims, keep, flag, raw, sems):
    chan_count, _, _ = sky.shape
    turns = rims.shape[0]
    first = towards(chan_count, turns)
    copies = [pltpu.make_async_copy(flags, flag, sems.at[turns])]
    for turn in range(turns):
        source = sky.at[pl.ds(first[turn], RIM)]
        copies.append(pltpu.make_async_copy(source, raw.at[turn], sems.at[turn]))
    run(copies)
    block = lax.axis_index("chan")
    before = (block > 0).astype(jnp.int32)
    after = (block < lax.axis_size("chan") - 1).astype(jnp.int32)
    factors = [before] * RIM + [1 - flag[c] for c in range(chan_count)] + [after] * RIM
    for i, factor in enumerate(factors):
        keep[i : i + 1, :] = jnp.full((1, LANES), factor.astype(f32), f32)
    for turn in range(turns):
        for i in range(RIM):
            factor = (1 - flag[first[turn] + i]).astype(f32)
            rims[turn, i] = (raw[turn, i].astype(f32) * factor).astype(bf16)


def load_kernel(sky, mid_in, edge_in, matrix_in, own, mid_band, edge_band, matrix, sems):
    run(
        [
            pltpu.make_async_copy(sky, own, sems.at[0]),
            pltpu.make_async_copy(matrix_in, matrix, sems.at[1]),
            pltpu.make_async_copy(mid_in, mid_band, sems.at[2]),
            pltpu.make_async_copy(edge_in, edge_band, sems.at[3]),
        ]
    )


def corner_kernel(n_rows, keep, first_pair, second_pair, corners, lasts):
    n_cols = first_pair.shape[2]
    chan_count = keep.shape[0] - 2 * RIM
    split = first_pair.shape[0] < chan_count
    for pair, halo in enumerate((first_pair, second_pair)):
        last = lasts.at[pair]
        if split:
            unpack(pair, n_rows, halo, last)
        for turn, first in enumerate(towards(chan_count, corners.shape[0])):
            for i in range(RIM):
                factor = wide(keep, RIM + first + i)
                for l in range(0, n_cols, LANES):
                    cols = slice(l, l + LANES)
                    value = halo_tile(halo, last, first + i, cols, split and i == RIM - 1)
                    corners[turn, pair * RIM + i, :, cols] = (value * factor).astype(bf16)


def middle_kernel(
    keep, sky, rim, row_band, matrix, spec, spec_exact, spec_squares, smooth, squares, sums, rowwise, acc
):
    chan_count, n_rows, n_cols = sky.shape
    per = n_rows - 2 * EDGE

    @pl.loop(0, n_rows // EDGE)
    def _(t):
        rows = pl.ds(pl.multiple_of(t * EDGE, EDGE), EDGE)
        for lane in range(0, n_cols, LANES):
            cols = slice(lane, lane + LANES)
            x = [rim[0, i, rows, cols] for i in range(RIM)]
            x += [sky[c, rows, cols] for c in range(chan_count)]
            x += [rim[rim.shape[0] - 1, i, rows, cols] for i in range(RIM)]
            x = [value.astype(f32) * wide(keep, i) for i, value in enumerate(x)]
            for c, both in means(x):
                for w in range(2):
                    spec[w, c, rows, cols] = both[w]

    group = 4

    @pl.loop(0, chan_count // group)
    def _(g):
        for w in range(2):

            def plane(c):
                value = spec[w, c]
                exact = value.astype(f32)
                square = exact * exact
                spec_exact[w, c] = exact
                spec_squares[w, c] = square
                acc[spectral_slot(chan_count, w, c)] = fold(square)
                return value

            c = [g * group + i for i in range(group)]
            row_pass(row_band[...], plane, rowwise, c, group, w * chan_count + g * group)

    def put(f, slot, values):
        w, c = slot // chan_count, slot % chan_count
        target = smooth_slot(chan_count, w, f, c)
        put_tiles(smooth, squares, acc, f, slot * per, target, values)

    column_pass(rowwise, matrix, 2 * chan_count, put)
    sums[...] = jnp.sum(acc[...], axis=1)


def edge_kernel(pairs, turns, rims, *refs):
    refs = list(refs)

    def take(count):
        taken = refs[:count]
        del refs[:count]
        return taken

    (keep,) = take(1)
    halos = take(len(pairs))
    corners = take(1)[0] if rims else None
    spec, row_band, matrix, sums = take(4)
    if rims:
        take(2 * len(pairs))
    outs = [take(2) for _ in pairs]
    sums_out, rowwise, acc, frame, lasts = refs
    chan_count, n_rows, n_cols = spec.shape[1:]
    near = frame.shape[2] - EDGE
    groups = [rest(chan_count, turns) + (None,)]
    if rims:
        groups = [(first, RIM, turn) for turn, first in enumerate(towards(chan_count, turns))]

    planes, taps = [], []
    for side, pair in enumerate(pairs):
        at = pair_rows(n_rows, pair)
        inside = pl.multiple_of(jnp.where(at == 0, 0, n_rows - near), EDGE)
        taps.append(row_band[jnp.where(at == 0, 0, 1)])
        halo, last = halos[side], lasts.at[side]
        split = halo.shape[0] < chan_count
        if split:
            unpack(pair, n_rows, halo, last)
        for first, count, turn in groups:
            may_start = [0, RIM] if turn is None else [0, chan_count - RIM]
            base = len(planes)
            planes += [(side, first + i) for i in range(count)]
            for lane in range(0, n_cols, LANES):
                cols = slice(lane, lane + LANES)
                x = []
                for i in range(count + 2 * RIM):
                    c = first - RIM + i
                    may_be_last = split and chan_count - 1 + RIM - i in may_start
                    value = halo_tile(halo, last, c, cols, may_be_last)
                    if turn is not None and (i < RIM or i >= count + RIM):
                        at_rim = pair * RIM + (i if i < RIM else i - count - RIM)
                        other = corners[turns - 1 - turn, at_rim, :, cols]
                        own = jnp.logical_and(c >= 0, c < chan_count)
                        value = jnp.where(own, value, other.astype(f32))
                    x.append(value * wide(keep, RIM + c))
                for i, both in means(x):
                    for w in range(2):
                        frame[w, base + i, :EDGE, cols] = both[w]
            for w in range(2):
                inner = spec[w, pl.ds(first, count), pl.ds(inside, near), :]
                frame[w, base : base + count, EDGE:, :] = inner

    count = len(planes)
    each = count // len(pairs)
    for w in range(2):
        for side in range(len(pairs)):
            slots = list(range(side * each, (side + 1) * each))
            row_pass(taps[side], lambda i: frame[w, i], rowwise, slots, each, w * count + side * each)
    acc[...] = jnp.zeros_like(acc)

    def put(f, slot, values):
        w = slot // count
        side, c = planes[slot % count]
        start = pl.multiple_of((w * chan_count + c) * EDGE, EDGE)
        target = smooth_slot(chan_count, w, f, c) - 2 * chan_count
        put_tiles(*outs[side], acc, f, start, target, values, side > 0)

    column_pass(rowwise, matrix, 2 * count, put)
    before = sums[: 2 * chan_count, :]
    total = sums[2 * chan_count :, :] + jnp.sum(acc[...], axis=1)
    if rims:
        sums_out[...] = share(jnp.concatenate([before, total]), sums_out)
    else:
        sums_out[: 2 * chan_count, :] = before
        sums_out[2 * chan_count :, :] = total


def share(acc_sum, out):
    peers, width = out.shape
    slots = acc_sum.shape[0]
    if slots < width:
        acc_sum = jnp.concatenate([acc_sum, jnp.zeros((width - slots, LANES), f32)], axis=0)
    total = jnp.sum(acc_sum.T, axis=0, keepdims=True)
    return jnp.broadcast_to(total, (peers, width))


def spread(shared):
    total = jnp.sum(shared[...], axis=0, keepdims=True)
    return jnp.broadcast_to(total, (LANES, total.shape[1])).T


def clip_kernel(pixels, shared_in, spec, middle, edge_one, edge_two, shared, limit, acc):
    chan_count = spec.shape[1]
    rough = jnp.sqrt(spread(shared_in) / pixels + epsilon)
    limit[...] = (clip_level * rough) ** 2

    @pl.loop(0, chan_count)
    def _(c):
        def clipped(slot, parts):
            top = wide(limit, slot, 8)
            total = None
            for part in parts:
                for r in range(0, part.shape[0], 8):
                    for l in range(0, part.shape[1], LANES):
                        value = jnp.minimum(part[r : r + 8, l : l + LANES], top)
                        total = value if total is None else total + value
            acc[slot] = total

        for w in range(2):
            clipped(spectral_slot(chan_count, w, c), [spec[w, c]])
            for f in range(2):
                parts = []
                for source in (middle, edge_one, edge_two):
                    per = source.shape[1] // (2 * chan_count)
                    start = pl.multiple_of((w * chan_count + c) * per, per)
                    parts.append(source[f, pl.ds(start, per), :])
                clipped(smooth_slot(chan_count, w, f, c), parts)

    shared[...] = share(jnp.sum(acc[...], axis=1), shared)


def ratio_kernel(pixels, keep, shared_in, spec, middle, edge_one, edge_two, out, scale, staged, sems):
    chan_count, n_rows, n_cols = out.shape
    scale[...] = 1.0 / jnp.sqrt(spread(shared_in) / pixels + epsilon)
    for k in range(6):
        rows = slice(k * chan_count, (k + 1) * chan_count)
        scale[rows, :] = scale[rows, :] * keep[RIM : RIM + chan_count, :]
    parts = sems.shape[0]
    group = chan_count // parts
    tiles = [(middle, r, EDGE + r) for r in range(0, n_rows - 2 * EDGE, EDGE)]
    tiles += [(edge_one, 0, pair_rows(n_rows, 0)), (edge_two, 0, pair_rows(n_rows, 1))]

    def channel(c):
        factors = [
            [wide(scale, spectral_slot(chan_count, w, c))]
            + [wide(scale, smooth_slot(chan_count, w, f, c)) for f in range(2)]
            for w in range(2)
        ]
        for source, offset, row in tiles:
            rows = pl.ds(row, EDGE)
            per = source.shape[1] // (2 * chan_count)
            for l in range(0, n_cols, LANES):
                cols = slice(l, l + LANES)
                best = None
                for w in range(2):
                    start = pl.multiple_of((w * chan_count + c) * per + offset, EDGE)
                    values = [spec[w, c, rows, cols]]
                    values += [source[f, pl.ds(start, EDGE), cols] for f in range(2)]
                    for value, factor in zip(values, factors[w]):
                        value = value * factor
                        best = value if best is None else jnp.maximum(best, value)
                staged[c, rows, cols] = best.astype(bf16)

    copies = []
    for p in range(parts):
        pl.loop(p * group, (p + 1) * group)(channel)
        s = slice(p * group, (p + 1) * group)
        copies.append(pltpu.make_async_copy(staged.at[s], out.at[s], sems.at[p]))
        copies[-1].start()
    for copy in copies:
        copy.wait()


def specs(spaces):
    return [pl.BlockSpec(memory_space=s) for s in spaces]


def call(kernel, ins, outs, scratch, flops, out_space=VMEM, aliases={}):
    return pl.pallas_call(
        kernel,
        in_specs=specs(ins),
        out_specs=specs([out_space] * len(outs)),
        out_shape=[jax.ShapeDtypeStruct(s, d) for s, d in outs],
        scratch_shapes=scratch,
        input_output_aliases=aliases,
        compiler_params=pltpu.CompilerParams(vmem_limit_bytes=12 * 2**20),
        cost_estimate=pl.CostEstimate(flops=flops, bytes_accessed=2**20, transcendentals=0),
    )


def shards(sky_cube, chan_flags):
    chan_count, n_rows, n_cols = sky_cube.shape
    strips, blocks = lax.axis_size("strip"), lax.axis_size("chan")
    pixels = n_rows * strips * n_cols
    turns = 1 if blocks == 2 else 2
    slots = 6 * chan_count
    width = -(-slots // LANES) * LANES
    mid = n_rows - 2 * EDGE
    near = 2 * EDGE
    dma = pltpu.SemaphoreType.DMA

    own_rows = np.arange(n_rows)
    mid_band = constant(band(own_rows[EDGE : n_rows - EDGE], own_rows).reshape(2 * mid, n_rows))
    top = band(np.arange(EDGE), np.concatenate([np.arange(-EDGE, 0), np.arange(near)]))
    bottom = band(np.arange(near - EDGE, near), np.concatenate([np.arange(near, near + EDGE), np.arange(near)]))
    edge_band = constant(np.stack([top, bottom]).reshape(2, 2 * EDGE, EDGE + near))
    cols = np.arange(n_cols)
    taps = band(cols, cols).transpose(0, 2, 1)
    same = cols[:, None] // BLOCK == cols[None, :] // BLOCK
    starts = np.arange(0, n_cols, BLOCK)
    pieces = [(taps * same)[:, b : b + BLOCK, b : b + BLOCK] for b in starts]
    pieces += [(taps * ~same)[:, b : b + BLOCK, b : b + BLOCK] for b in starts[:-1] + LANES]
    matrix = constant(np.stack(pieces, axis=1))

    sky_cube, chan_flags, mid_band, edge_band, matrix = (
        pltpu.with_memory_space_constraint(v, HBM)
        for v in (sky_cube, chan_flags, mid_band, edge_band, matrix)
    )

    edge_rows = ((packed(chan_count), EDGE, n_cols), bf16)
    last_rows = (2, EDGE, n_cols)
    first_pair, second_pair = call(
        pick_kernel,
        [HBM],
        [edge_rows, edge_rows],
        [VMEM(last_rows, bf16), VMEM(last_rows, f32), dma((4,))],
        10**6,
    )(sky_cube)

    evens = [(i, i + 1) for i in range(0, strips - 1, 2)]
    odds = [(i, i + 1) for i in range(1, strips - 1, 2)]
    evens, odds = (p + [(b, a) for a, b in p] for p in (evens, odds))
    first_pair = lax.ppermute(first_pair, "strip", evens)
    second_pair = lax.ppermute(second_pair, "strip", odds)

    forth = [(i, i + 1) for i in range(blocks - 1)]
    back = [(j, i) for i, j in forth]
    moves = [forth + back] if turns == 1 else [forth, back]

    def across(payload):
        sent = [lax.ppermute(payload[i : i + 1], "chan", p) for i, p in enumerate(moves)]
        return jnp.concatenate(sent)

    rims, keep = call(
        rim_kernel,
        [HBM, HBM],
        [((turns, RIM, n_rows, n_cols), bf16), ((chan_count + 2 * RIM, LANES), f32)],
        [
            SMEM((chan_count,), jnp.int32),
            VMEM((turns, RIM, n_rows, n_cols), bf16),
            dma((turns + 1,)),
        ],
        10**6,
    )(chan_flags, sky_cube)
    rim = across(rims)
    own, mid_band, edge_band, matrix = call(
        load_kernel,
        [HBM] * 4,
        [(v.shape, bf16) for v in (sky_cube, mid_band, edge_band, matrix)],
        [dma((4,))],
        10**6,
    )(sky_cube, mid_band, edge_band, matrix)

    mid_out = ((2, 2 * chan_count * mid, n_cols), f32)
    sums_out = ((slots, LANES), f32)
    spec, spec_exact, spec_squares, middle, middle_squares, sums = call(
        middle_kernel,
        [VMEM] * 5,
        [
            ((2, chan_count, n_rows, n_cols), bf16),
            ((2, chan_count, n_rows, n_cols), f32),
            ((2, chan_count, n_rows, n_cols), f32),
            mid_out,
            mid_out,
            sums_out,
        ],
        [VMEM(mid_out[0], bf16), VMEM((slots, 8, LANES), f32)],
        2 * 10**9,
    )(keep, own, rim, mid_band, matrix)

    (corners,) = call(
        functools.partial(corner_kernel, n_rows),
        [VMEM] * 3,
        [((turns, 2 * RIM, EDGE, n_cols), bf16)],
        [VMEM(last_rows, f32)],
        10**6,
    )(keep, first_pair, second_pair)
    corners = across(corners)

    def edge(pairs, rims, *args):
        count = turns * RIM if rims else chan_count - turns * RIM
        count *= len(pairs)
        outs = [((2, 2 * chan_count * EDGE, n_cols), f32)] * (2 * len(pairs))
        in_place = {len(args) - len(outs) + i: i for i in range(len(outs))}
        return call(
            functools.partial(edge_kernel, pairs, turns, rims),
            [VMEM] * len(args),
            outs + [((strips, width), f32) if rims else sums_out],
            [
                VMEM((2, 2 * count * EDGE, n_cols), bf16),
                VMEM((slots - 2 * chan_count, 8, LANES), f32),
                VMEM((2, count, EDGE + near, n_cols), bf16),
                VMEM((len(pairs), EDGE, n_cols), f32),
            ],
            10**9,
            aliases=in_place if rims else {},
        )(*args)

    shared_args = (spec, edge_band, matrix)
    *two, sums = edge((1,), False, keep, second_pair, *shared_args, sums)
    *one, sums = edge((0,), False, keep, first_pair, *shared_args, sums)
    args = (keep, first_pair, second_pair, corners, *shared_args, sums)
    edge_one, one_squares, edge_two, two_squares, shared = edge((0, 1), True, *args, *one, *two)

    shared = lax.all_to_all(shared, "strip", 0, 0, tiled=True)
    (shared,) = call(
        functools.partial(clip_kernel, pixels),
        [VMEM] * 5,
        [((strips, width), f32)],
        [VMEM((width, LANES), f32), VMEM((slots, 8, LANES), f32)],
        10**8,
    )(shared, spec_squares, middle_squares, one_squares, two_squares)
    shared = lax.all_to_all(shared, "strip", 0, 0, tiled=True)
    (out,) = call(
        functools.partial(ratio_kernel, pixels),
        [VMEM] * 6,
        [((chan_count, n_rows, n_cols), bf16)],
        [VMEM((width, LANES), f32), VMEM((chan_count, n_rows, n_cols), bf16), dma((4,))],
        10**8,
        HBM,
    )(keep, shared, spec_exact, middle, edge_one, edge_two)
    return out


def solution(mesh):
    in_specs = (P("chan", "strip", "groups"), P("chan"))
    out_specs = P("chan", "strip", "groups")
    return jax.shard_map(shards, mesh=mesh, in_specs=in_specs, out_specs=out_specs, check_vma=False)
```

profile of v0, /device:TPU:0, one launch (start us, length us, event | category | flops | bytes accessed | tf_op | source)
XLA Modules:
  0.0 44.0 jit_solution(8554066067316574371)
XLA Ops:
  0.0 1.0 %shard_map.55 = (bf16[1,3,64,512]{3,2,1,0:T(8,128)(2,1)S(1)}, f32[22,128]{1,0:T(8,128)S(1)}) custom-call(s32[16]{0:T(128)} %flags.1, bf16[16,64,512]{2,1,0:T(8,128)(2,1)} %sky.5), custom_call_target="tpu_custom_call" | custom-call | flops 1000000 | bytes 1048576 | tf_op jit(solution)/shard_map/pallas_call | solution.py:529
  1.0 0.6 %collective-permute-start.3 = (bf16[1,3,64,512]{3,2,1,0:T(8,128)(2,1)S(1)}, bf16[1,3,64,512]{3,2,1,0:T(8,128)(2,1)S(1)}, u32[]{:S(2)}, u32[]{:S(2)}) collective-permute-start(bf16[1,3,64,512]{3,2,1,0:T(8,128)(2,1)S(1)} %get-tuple-element.34), channel_id=1, source_target_pairs={{0,1},{1,0},{2,3},{3,2},{4,5},{5,4},{6,7},{7,6},{8,9},{9,8},{10,11... | collective-permute-start | bytes 589832 | tf_op jit(solution)/shard_map/ppermute | solution.py:526
  1.6 1.2 %shard_map.56 = (bf16[15,16,512]{2,1,0:T(8,128)(2,1)S(1)}, bf16[15,16,512]{2,1,0:T(8,128)(2,1)S(1)}) custom-call(bf16[16,64,512]{2,1,0:T(8,128)(2,1)} %sky.5), custom_call_target="tpu_custom_call" | custom-call | flops 1000000 | bytes 1048576 | tf_op jit(solution)/shard_map/pallas_call | solution.py:507
  2.7 2.6 %collective-permute-start = (bf16[15,16,512]{2,1,0:T(8,128)(2,1)S(1)}, bf16[15,16,512]{2,1,0:T(8,128)(2,1)S(1)}, u32[]{:S(2)}, u32[]{:S(2)}) collective-permute-start(bf16[15,16,512]{2,1,0:T(8,128)(2,1)S(1)} %get-tuple-element.31), channel_id=1, source_target_pairs={{0,2},{4,6},{8,10},{12,14},{2,0},{6,4},{10,8},{14,12},{1,3},{5,7},... | collective-permute-start | bytes 737288 | tf_op jit(solution)/shard_map/ppermute | solution.py:518
  5.3 0.7 %collective-permute-start.1 = (bf16[15,16,512]{2,1,0:T(8,128)(2,1)S(1)}, bf16[15,16,512]{2,1,0:T(8,128)(2,1)S(1)}, u32[]{:S(2)}, u32[]{:S(2)}) collective-permute-start(bf16[15,16,512]{2,1,0:T(8,128)(2,1)S(1)} %get-tuple-element.32), channel_id=1, source_target_pairs={{2,4},{6,8},{10,12},{4,2},{8,6},{12,10},{3,5},{7,9},{11,13},{5,3},... | collective-permute-start | bytes 737288 | tf_op jit(solution)/shard_map/ppermute | solution.py:519
  6.0 1.5 %shard_map.58 = (bf16[16,64,512]{2,1,0:T(8,128)(2,1)S(1)}, bf16[64,64]{1,0:T(8,128)(2,1)S(1)}, bf16[2,32,48]{2,1,0:T(8,128)(2,1)S(1)}, bf16[2,3,256,256]{3,2,1,0:T(8,128)(2,1)S(1)}) custom-call(bf16[16,64,512]{2,1,0:T(8,128)(2,1)} %sky.5, bf16[64,64]{1,0:T(8,128)(2,1)} %constant.9.mid_in, bf16[2,32,48]{2,1,0:T(8,128)(2,1)} %constant.10.edge_in, ...), custom_call_target="tpu_custom_call" | custom-call | flops 1000000 | bytes 1048576 | tf_op jit(solution)/shard_map/pallas_call | solution.py:541
  7.5 0.0 collective-permute-done.3.rim
  7.5 3.0 %shard_map.59 = (bf16[2,16,64,512]{3,2,1,0:T(8,128)(2,1)S(1)}, f32[2,16,64,512]{3,2,1,0:T(8,128)S(1)}, f32[2,16,64,512]{3,2,1,0:T(8,128)S(1)}, f32[2,1024,512]{2...) custom-call(f32[22,128]{1,0:T(8,128)S(1)} %get-tuple-element.30.keep.refs_0_, ...), custom_call_target="tpu_custom_call" | custom-call | flops 2000000000 | bytes 1048576 | tf_op jit(solution)/shard_map/pallas_call | solution.py:551
  10.5 6.0 %collective-permute-done.first_pair.refs_1_ = bf16[15,16,512]{2,1,0:T(8,128)(2,1)S(1)} collective-permute-done((bf16[15,16,512]{2,1,0:T(8,128)(2,1)S(1)}, bf16[15,16,512]{2,1,0:T(8,128)(2,1)S(1)}, u32[]{:S(2)}, u32[]{:S(2)}) %collective-permute-start) | collective-permute-done | bytes 245792 | tf_op jit(solution)/shard_map/ppermute | solution.py:518
  16.4 0.0 collective-permute-done.1.second_pair.refs_1_.refs_2_
  16.4 0.1 shard_map.57
  16.5 0.1 collective-permute-start.2
  16.6 1.0 %shard_map.60 = (f32[2,512,512]{2,1,0:T(8,128)S(1)}, f32[2,512,512]{2,1,0:T(8,128)S(1)}, f32[96,128]{1,0:T(8,128)S(1)}) custom-call(f32[22,128]{1,0:T(8,128)S(1)} %get-tuple-element.30.keep.refs_0_, bf16[15,16,512]{2,1,0:T(8,128)(2,1)S(1)} %collective-permute-done.1.second_pair.refs_1_.refs_2_, ...), custom_call_target="tpu_custom_call" | custom-call | flops 1000000000 | bytes 1048576 | tf_op jit(solution)/shard_map/pallas_call | solution.py:580
  17.6 1.0 %shard_map.61 = (f32[2,512,512]{2,1,0:T(8,128)S(1)}, f32[2,512,512]{2,1,0:T(8,128)S(1)}, f32[96,128]{1,0:T(8,128)S(1)}) custom-call(f32[22,128]{1,0:T(8,128)S(1)} %get-tuple-element.30.keep.refs_0_, bf16[15,16,512]{2,1,0:T(8,128)(2,1)S(1)} %collective-permute-done.first_pair.refs_1_, bf16[2,16,64,512]{3,2,1,0:T(8,128)(2,1)S(1)} %get-tuple-element.37.refs_2_.refs_4_, ...), custom_call_target="tpu_custom_call" | custom-call | flops 1000000000 | bytes 1048576 | tf_op jit(solution)/shard_map/pallas_call | solution.py:580
  18.6 0.0 collective-permute-done.2.refs_3_
  18.6 0.8 %shard_map.62 = (f32[2,512,512]{2,1,0:T(8,128)S(1)}, f32[2,512,512]{2,1,0:T(8,128)S(1)}, f32[2,512,512]{2,1,0:T(8,128)S(1)}, f32[2,512,512]{2,1,0:T(8,128)S(1)}, f32[8,128]{1,0:T(8,128)S(1)}) custom-call(f32[22,128]{1,0:T(8,128)S(1)} %get-tuple-element.30.keep.refs_0_, ...), custom_call_target="tpu_custom_call", output_to_operand_aliasing={{0}: (8, {}), {1}: (9, {}), {2}: (10, {}), {3}: (11, {})} | custom-call | flops 1000000000 | bytes 1048576 | tf_op jit(solution)/shard_map/pallas_call | solution.py:580
  19.4 12.2 %all_to_all.22 = f32[8,1,128]{2,1,0:T(1,128)S(1)} all-to-all(f32[8,1,128]{2,1,0:T(1,128)S(1)} %bitcast.11), channel_id=1, replica_groups=mesh['groups'=2,'strip'=8,'chan'=2] {'strip'}, dimensions={0} | all-to-all | bytes 8192 | tf_op jit(solution)/shard_map/all_to_all | solution.py:600
  31.6 1.6 %shard_map.63 = f32[8,128]{1,0:T(8,128)S(1)} custom-call(f32[8,128]{1,0:T(8,128)S(1)} %bitcast.9, f32[2,16,64,512]{3,2,1,0:T(8,128)S(1)} %get-tuple-element.47.spec, f32[2,1024,512]{2,1,0:T(8,128)S(1)} %get-tuple-element.48.middle, f32[2,512,512]{2,1,0:T(8,128)S(1)} %get-tuple-element.49.edge_one, f32[2,512,512]{2,1,0:T(8,128)S(1)} %get-tuple-element.50.edge_two), custom_call_target="tpu_custom_call" | custom-call | flops 100000000 | bytes 1048576 | tf_op jit(solution)/shard_map/pallas_call | solution.py:601
  33.2 8.9 %all_to_all.23 = f32[8,1,128]{2,1,0:T(1,128)S(1)} all-to-all(f32[8,1,128]{2,1,0:T(1,128)S(1)} %bitcast.10), channel_id=1, replica_groups=mesh['groups'=2,'strip'=8,'chan'=2] {'strip'}, dimensions={0} | all-to-all | bytes 8192 | tf_op jit(solution)/shard_map/all_to_all | solution.py:608
  42.0 2.0 %shard_map.64 = bf16[16,64,512]{2,1,0:T(8,128)(2,1)} custom-call(f32[22,128]{1,0:T(8,128)S(1)} %get-tuple-element.30.keep.refs_0_, f32[8,128]{1,0:T(8,128)S(1)} %bitcast.8, f32[2,16,64,512]{3,2,1,0:T(8,128)S(1)} %get-tuple-element.51.spec, f32[2,1024,512]{2,1,0:T(8,128)S(1)} %get-tuple-element.52.middle, f32[2,512,512]{2,1,0:T(8,128)S(1)} %get-tuple-element.53.edge_one, ...), custom_call_target="tpu_custom_call" | custom-call | flops 100000000 | bytes 1048576 | tf_op jit(solution)/shard_map/pallas_call | solution.py:609
Async XLA Ops:
  1.0 6.5 %collective-permute-start.3 = (bf16[1,3,64,512]{3,2,1,0:T(8,128)(2,1)S(1)}, bf16[1,3,64,512]{3,2,1,0:T(8,128)(2,1)S(1)}, u32[]{:S(2)}, u32[]{:S(2)}) collective-permute-start(bf16[1,3,64,512]{3,2,1,0:T(8,128)(2,1)S(1)} %get-tuple-element.34), channel_id=1, source_target_pairs={{0,1},{1,0},{2,3},{3,2},{4,5},{5,4},{6,7},{7,6},{8,9},{9,8},{10,11... | collective-permute-start | bytes 589832 | tf_op jit(solution)/shard_map/ppermute | solution.py:526
  2.7 13.7 %collective-permute-start = (bf16[15,16,512]{2,1,0:T(8,128)(2,1)S(1)}, bf16[15,16,512]{2,1,0:T(8,128)(2,1)S(1)}, u32[]{:S(2)}, u32[]{:S(2)}) collective-permute-start(bf16[15,16,512]{2,1,0:T(8,128)(2,1)S(1)} %get-tuple-element.31), channel_id=1, source_target_pairs={{0,2},{4,6},{8,10},{12,14},{2,0},{6,4},{10,8},{14,12},{1,3},{5,7},... | collective-permute-start | bytes 737288 | tf_op jit(solution)/shard_map/ppermute | solution.py:518
  5.3 11.1 %collective-permute-start.1 = (bf16[15,16,512]{2,1,0:T(8,128)(2,1)S(1)}, bf16[15,16,512]{2,1,0:T(8,128)(2,1)S(1)}, u32[]{:S(2)}, u32[]{:S(2)}) collective-permute-start(bf16[15,16,512]{2,1,0:T(8,128)(2,1)S(1)} %get-tuple-element.32), channel_id=1, source_target_pairs={{2,4},{6,8},{10,12},{4,2},{8,6},{12,10},{3,5},{7,9},{11,13},{5,3},... | collective-permute-start | bytes 737288 | tf_op jit(solution)/shard_map/ppermute | solution.py:519
  16.5 2.1 %collective-permute-start.2 = (bf16[1,6,16,512]{3,2,1,0:T(8,128)(2,1)S(1)}, bf16[1,6,16,512]{3,2,1,0:T(8,128)(2,1)S(1)}, u32[]{:S(2)}, u32[]{:S(2)}) collective-permute-start(bf16[1,6,16,512]{3,2,1,0:T(8,128)(2,1)S(1)} %shard_map.57), channel_id=1, source_target_pairs={{0,1},{1,0},{2,3},{3,2},{4,5},{5,4},{6,7},{7,6},{8,9},{9,8},{10,11... | collective-permute-start | bytes 294920 | tf_op jit(solution)/shard_map/ppermute | solution.py:526
where the time goes:
time: 44.3 us; the launch traced here: 44 us
  blocking collectives  21 us (47%)
  Pallas kernels  13 us (29%)
  waiting for transfers between devices  5.98 us (13%)
  starting transfers between devices  3.86 us (9%)
    all_to_all x2, blocking collectives, shards(): shared = lax.all_to_all(shared, 'strip', 0, 0, tiled=True)  21 us
    ppermute x1, waiting for transfers between devices, shards(): first_pair = lax.ppermute(first_pair, 'strip', evens)  5.97 us
    pallas_call x1, Pallas kernels, shards(): call(middle_kernel, [VMEM] * 5, [((2, chan_count, n_rows, n_cols), bf16),...  2.97 us
    pallas_call x3, Pallas kernels, edge(): call(functools.partial(edge_kernel, pairs, turns, rims), [VMEM] * len(arg...  2.77 us
    ppermute x1, starting transfers between devices, shards(): first_pair = lax.ppermute(first_pair, 'strip', evens)  2.57 us
    pallas_call x1, Pallas kernels, shards(): call(functools.partial(ratio_kernel, pixels), [VMEM] * 6, [((chan_count,...  1.97 us
    pallas_call x1, Pallas kernels, shards(): call(functools.partial(clip_kernel, pixels), [VMEM] * 5, [((strips, width...  1.57 us
    pallas_call x1, Pallas kernels, shards(): call(load_kernel, [HBM] * 4, [(v.shape, bf16) for v in (sky_cube, mid_ban...  1.49 us
  transfers between devices with their start and end apart: 4, of which 1 were waited for; matrix products, arithmetic and copies ran while one was open for 0% of the time, Pallas kernels for 17%

commit v1 on v0

--- a/solution.py
+++ b/solution.py
@@ -290,7 +290,7 @@
     sums[...] = jnp.sum(acc[...], axis=1)
 
 
-def edge_kernel(pairs, turns, rims, *refs):
+def edge_kernel(pairs, turns, rims, given, *refs):
     refs = list(refs)
 
     def take(count):
@@ -301,11 +301,17 @@
     (keep,) = take(1)
     halos = take(len(pairs))
     corners = take(1)[0] if rims else None
+    lasts = take(1)[0] if given else None
     spec, row_band, matrix, sums = take(4)
     if rims:
         take(2 * len(pairs))
     outs = [take(2) for _ in pairs]
-    sums_out, rowwise, acc, frame, lasts = refs
+    if lasts is None:
+        lasts = refs.pop()
+        unpacked = False
+    else:
+        unpacked = True
+    sums_out, rowwise, acc, frame = refs
     chan_count, n_rows, n_cols = spec.shape[1:]
     near = frame.shape[2] - EDGE
     groups = [rest(chan_count, turns) + (None,)]
@@ -317,9 +323,9 @@
         at = pair_rows(n_rows, pair)
         inside = pl.multiple_of(jnp.where(at == 0, 0, n_rows - near), EDGE)
         taps.append(row_band[jnp.where(at == 0, 0, 1)])
-        halo, last = halos[side], lasts.at[side]
+        halo, last = halos[side], lasts.at[pair if unpacked else side]
         split = halo.shape[0] < chan_count
-        if split:
+        if split and not unpacked:
             unpack(pair, n_rows, halo, last)
         for first, count, turn in groups:
             may_start = [0, RIM] if turn is None else [0, chan_count - RIM]
@@ -563,39 +569,39 @@
         2 * 10**9,
     )(keep, own, rim, mid_band, matrix)
 
-    (corners,) = call(
+    corners, lasts = call(
         functools.partial(corner_kernel, n_rows),
         [VMEM] * 3,
-        [((turns, 2 * RIM, EDGE, n_cols), bf16)],
-        [VMEM(last_rows, f32)],
+        [((turns, 2 * RIM, EDGE, n_cols), bf16), (last_rows, f32)],
+        [],
         10**6,
     )(keep, first_pair, second_pair)
     corners = across(corners)
 
-    def edge(pairs, rims, *args):
+    def edge(pairs, rims, given, *args):
         count = turns * RIM if rims else chan_count - turns * RIM
         count *= len(pairs)
         outs = [((2, 2 * chan_count * EDGE, n_cols), f32)] * (2 * len(pairs))
         in_place = {len(args) - len(outs) + i: i for i in range(len(outs))}
         return call(
-            functools.partial(edge_kernel, pairs, turns, rims),
+            functools.partial(edge_kernel, pairs, turns, rims, given),
             [VMEM] * len(args),
             outs + [((strips, width), f32) if rims else sums_out],
             [
                 VMEM((2, 2 * count * EDGE, n_cols), bf16),
                 VMEM((slots - 2 * chan_count, 8, LANES), f32),
                 VMEM((2, count, EDGE + near, n_cols), bf16),
-                VMEM((len(pairs), EDGE, n_cols), f32),
-            ],
+            ]
+            + ([] if given else [VMEM((len(pairs), EDGE, n_cols), f32)]),
             10**9,
             aliases=in_place if rims else {},
         )(*args)
 
     shared_args = (spec, edge_band, matrix)
-    *two, sums = edge((1,), False, keep, second_pair, *shared_args, sums)
-    *one, sums = edge((0,), False, keep, first_pair, *shared_args, sums)
-    args = (keep, first_pair, second_pair, corners, *shared_args, sums)
-    edge_one, one_squares, edge_two, two_squares, shared = edge((0, 1), True, *args, *one, *two)
+    *two, sums = edge((1,), False, False, keep, second_pair, *shared_args, sums)
+    *one, sums = edge((0,), False, True, keep, first_pair, lasts, *shared_args, sums)
+    args = (keep, first_pair, second_pair, corners, lasts, *shared_args, sums)
+    edge_one, one_squares, edge_two, two_squares, shared = edge((0, 1), True, True, *args, *one, *two)
 
     shared = lax.all_to_all(shared, "strip", 0, 0, tiled=True)
     (shared,) = call(

time: 44.3 us -> 44.1 us (level)
  no operation moved by 1% of the time
where the time goes in v1:
time: 44.1 us; the launch traced here: 43.9 us
  blocking collectives  21 us (48%)
  Pallas kernels  12.9 us (29%)
  waiting for transfers between devices  5.99 us (14%)
  starting transfers between devices  3.86 us (9%)
    all_to_all x2, blocking collectives, shards(): shared = lax.all_to_all(shared, 'strip', 0, 0, tiled=True)  21 us
    ppermute x1, waiting for transfers between devices, shards(): first_pair = lax.ppermute(first_pair, 'strip', evens)  5.98 us
    pallas_call x1, Pallas kernels, shards(): call(middle_kernel, [VMEM] * 5, [((2, chan_count, n_rows, n_cols), bf16),...  2.96 us
    pallas_call x3, Pallas kernels, edge(): call(functools.partial(edge_kernel, pairs, turns, rims, given), [VMEM] *...  2.66 us
    ppermute x1, starting transfers between devices, shards(): first_pair = lax.ppermute(first_pair, 'strip', evens)  2.57 us
    pallas_call x1, Pallas kernels, shards(): call(functools.partial(ratio_kernel, pixels), [VMEM] * 6, [((chan_count,...  1.97 us
    pallas_call x1, Pallas kernels, shards(): call(functools.partial(clip_kernel, pixels), [VMEM] * 5, [((strips, width...  1.57 us
    pallas_call x1, Pallas kernels, shards(): call(load_kernel, [HBM] * 4, [(v.shape, bf16) for v in (sky_cube, mid_ban...  1.49 us
  transfers between devices with their start and end apart: 4, of which 1 were waited for; matrix products, arithmetic and copies ran while one was open for 0% of the time, Pallas kernels for 17%

profile of v1, /device:TPU:0, one launch (start us, length us, event | category | flops | bytes accessed | tf_op | source)
XLA Modules:
  0.0 43.9 jit_solution(6724521325873072293)
XLA Ops:
  0.0 1.0 %shard_map.55 = (bf16[1,3,64,512]{3,2,1,0:T(8,128)(2,1)S(1)}, f32[22,128]{1,0:T(8,128)S(1)}) custom-call(s32[16]{0:T(128)} %flags.1, bf16[16,64,512]{2,1,0:T(8,128)(2,1)} %sky.5), custom_call_target="tpu_custom_call" | custom-call | flops 1000000 | bytes 1048576 | tf_op jit(solution)/shard_map/pallas_call | solution.py:535
  1.0 0.6 %collective-permute-start.3 = (bf16[1,3,64,512]{3,2,1,0:T(8,128)(2,1)S(1)}, bf16[1,3,64,512]{3,2,1,0:T(8,128)(2,1)S(1)}, u32[]{:S(2)}, u32[]{:S(2)}) collective-permute-start(bf16[1,3,64,512]{3,2,1,0:T(8,128)(2,1)S(1)} %get-tuple-element.38), channel_id=1, source_target_pairs={{0,1},{1,0},{2,3},{3,2},{4,5},{5,4},{6,7},{7,6},{8,9},{9,8},{10,11... | collective-permute-start | bytes 589832 | tf_op jit(solution)/shard_map/ppermute | solution.py:532
  1.6 1.2 %shard_map.56 = (bf16[15,16,512]{2,1,0:T(8,128)(2,1)S(1)}, bf16[15,16,512]{2,1,0:T(8,128)(2,1)S(1)}) custom-call(bf16[16,64,512]{2,1,0:T(8,128)(2,1)} %sky.5), custom_call_target="tpu_custom_call" | custom-call | flops 1000000 | bytes 1048576 | tf_op jit(solution)/shard_map/pallas_call | solution.py:513
  2.7 2.6 %collective-permute-start = (bf16[15,16,512]{2,1,0:T(8,128)(2,1)S(1)}, bf16[15,16,512]{2,1,0:T(8,128)(2,1)S(1)}, u32[]{:S(2)}, u32[]{:S(2)}) collective-permute-start(bf16[15,16,512]{2,1,0:T(8,128)(2,1)S(1)} %get-tuple-element.33), channel_id=1, source_target_pairs={{0,2},{4,6},{8,10},{12,14},{2,0},{6,4},{10,8},{14,12},{1,3},{5,7},... | collective-permute-start | bytes 737288 | tf_op jit(solution)/shard_map/ppermute | solution.py:524
  5.3 0.7 %collective-permute-start.1 = (bf16[15,16,512]{2,1,0:T(8,128)(2,1)S(1)}, bf16[15,16,512]{2,1,0:T(8,128)(2,1)S(1)}, u32[]{:S(2)}, u32[]{:S(2)}) collective-permute-start(bf16[15,16,512]{2,1,0:T(8,128)(2,1)S(1)} %get-tuple-element.34), channel_id=1, source_target_pairs={{2,4},{6,8},{10,12},{4,2},{8,6},{12,10},{3,5},{7,9},{11,13},{5,3},... | collective-permute-start | bytes 737288 | tf_op jit(solution)/shard_map/ppermute | solution.py:525
  6.0 1.5 %shard_map.58 = (bf16[16,64,512]{2,1,0:T(8,128)(2,1)S(1)}, bf16[64,64]{1,0:T(8,128)(2,1)S(1)}, bf16[2,32,48]{2,1,0:T(8,128)(2,1)S(1)}, bf16[2,3,256,256]{3,2,1,0:T(8,128)(2,1)S(1)}) custom-call(bf16[16,64,512]{2,1,0:T(8,128)(2,1)} %sky.5, bf16[64,64]{1,0:T(8,128)(2,1)} %constant.9.mid_in, bf16[2,32,48]{2,1,0:T(8,128)(2,1)} %constant.10.edge_in, ...), custom_call_target="tpu_custom_call" | custom-call | flops 1000000 | bytes 1048576 | tf_op jit(solution)/shard_map/pallas_call | solution.py:547
  7.5 0.0 collective-permute-done.3.rim
  7.5 3.0 %shard_map.59 = (bf16[2,16,64,512]{3,2,1,0:T(8,128)(2,1)S(1)}, f32[2,16,64,512]{3,2,1,0:T(8,128)S(1)}, f32[2,16,64,512]{3,2,1,0:T(8,128)S(1)}, f32[2,1024,512]{2...) custom-call(f32[22,128]{1,0:T(8,128)S(1)} %get-tuple-element.32.keep.refs_0_, ...), custom_call_target="tpu_custom_call" | custom-call | flops 2000000000 | bytes 1048576 | tf_op jit(solution)/shard_map/pallas_call | solution.py:557
  10.5 6.0 %collective-permute-done.first_pair.refs_1_ = bf16[15,16,512]{2,1,0:T(8,128)(2,1)S(1)} collective-permute-done((bf16[15,16,512]{2,1,0:T(8,128)(2,1)S(1)}, bf16[15,16,512]{2,1,0:T(8,128)(2,1)S(1)}, u32[]{:S(2)}, u32[]{:S(2)}) %collective-permute-start) | collective-permute-done | bytes 245792 | tf_op jit(solution)/shard_map/ppermute | solution.py:524
  16.4 0.0 collective-permute-done.1.second_pair.refs_1_.refs_2_
  16.4 0.1 shard_map.57
  16.5 0.1 collective-permute-start.2
  16.6 1.0 %shard_map.60 = (f32[2,512,512]{2,1,0:T(8,128)S(1)}, f32[2,512,512]{2,1,0:T(8,128)S(1)}, f32[96,128]{1,0:T(8,128)S(1)}) custom-call(f32[22,128]{1,0:T(8,128)S(1)} %get-tuple-element.32.keep.refs_0_, bf16[15,16,512]{2,1,0:T(8,128)(2,1)S(1)} %collective-permute-done.1.second_pair.refs_1_.refs_2_, ...), custom_call_target="tpu_custom_call" | custom-call | flops 1000000000 | bytes 1048576 | tf_op jit(solution)/shard_map/pallas_call | solution.py:586
  17.6 1.0 %shard_map.61 = (f32[2,512,512]{2,1,0:T(8,128)S(1)}, f32[2,512,512]{2,1,0:T(8,128)S(1)}, f32[96,128]{1,0:T(8,128)S(1)}) custom-call(f32[22,128]{1,0:T(8,128)S(1)} %get-tuple-element.32.keep.refs_0_, bf16[15,16,512]{2,1,0:T(8,128)(2,1)S(1)} %collective-permute-done.first_pair.refs_1_, f32[2,16,512]{2,1,0:T(8,128)S(1)} %get-tuple-element.36.refs_2_.refs_4_, ...), custom_call_target="tpu_custom_call" | custom-call | flops 1000000000 | bytes 1048576 | tf_op jit(solution)/shard_map/pallas_call | solution.py:586
  18.6 0.0 collective-permute-done.2.refs_3_
  18.6 0.7 %shard_map.62 = (f32[2,512,512]{2,1,0:T(8,128)S(1)}, f32[2,512,512]{2,1,0:T(8,128)S(1)}, f32[2,512,512]{2,1,0:T(8,128)S(1)}, f32[2,512,512]{2,1,0:T(8,128)S(1)}, f32[8,128]{1,0:T(8,128)S(1)}) custom-call(f32[22,128]{1,0:T(8,128)S(1)} %get-tuple-element.32.keep.refs_0_, ...), custom_call_target="tpu_custom_call", output_to_operand_aliasing={{0}: (9, {}), {1}: (10, {}), {2}: (11, {}), {3}: (12, {})} | custom-call | flops 1000000000 | bytes 1048576 | tf_op jit(solution)/shard_map/pallas_call | solution.py:586
  19.3 12.1 %all_to_all.22 = f32[8,1,128]{2,1,0:T(1,128)S(1)} all-to-all(f32[8,1,128]{2,1,0:T(1,128)S(1)} %bitcast.11), channel_id=1, replica_groups=mesh['groups'=2,'strip'=8,'chan'=2] {'strip'}, dimensions={0} | all-to-all | bytes 8192 | tf_op jit(solution)/shard_map/all_to_all | solution.py:606
  31.5 1.6 %shard_map.63 = f32[8,128]{1,0:T(8,128)S(1)} custom-call(f32[8,128]{1,0:T(8,128)S(1)} %bitcast.9, f32[2,16,64,512]{3,2,1,0:T(8,128)S(1)} %get-tuple-element.51.spec, f32[2,1024,512]{2,1,0:T(8,128)S(1)} %get-tuple-element.52.middle, f32[2,512,512]{2,1,0:T(8,128)S(1)} %get-tuple-element.53.edge_one, f32[2,512,512]{2,1,0:T(8,128)S(1)} %get-tuple-element.54.edge_two), custom_call_target="tpu_custom_call" | custom-call | flops 100000000 | bytes 1048576 | tf_op jit(solution)/shard_map/pallas_call | solution.py:607
  33.0 8.9 %all_to_all.23 = f32[8,1,128]{2,1,0:T(1,128)S(1)} all-to-all(f32[8,1,128]{2,1,0:T(1,128)S(1)} %bitcast.10), channel_id=1, replica_groups=mesh['groups'=2,'strip'=8,'chan'=2] {'strip'}, dimensions={0} | all-to-all | bytes 8192 | tf_op jit(solution)/shard_map/all_to_all | solution.py:614
  41.9 2.0 %shard_map.64 = bf16[16,64,512]{2,1,0:T(8,128)(2,1)} custom-call(f32[22,128]{1,0:T(8,128)S(1)} %get-tuple-element.32.keep.refs_0_, f32[8,128]{1,0:T(8,128)S(1)} %bitcast.8, f32[2,16,64,512]{3,2,1,0:T(8,128)S(1)} %get-tuple-element.55.spec, f32[2,1024,512]{2,1,0:T(8,128)S(1)} %get-tuple-element.56.middle, f32[2,512,512]{2,1,0:T(8,128)S(1)} %get-tuple-element.57.edge_one, ...), custom_call_target="tpu_custom_call" | custom-call | flops 100000000 | bytes 1048576 | tf_op jit(solution)/shard_map/pallas_call | solution.py:615
Async XLA Ops:
  1.0 6.5 %collective-permute-start.3 = (bf16[1,3,64,512]{3,2,1,0:T(8,128)(2,1)S(1)}, bf16[1,3,64,512]{3,2,1,0:T(8,128)(2,1)S(1)}, u32[]{:S(2)}, u32[]{:S(2)}) collective-permute-start(bf16[1,3,64,512]{3,2,1,0:T(8,128)(2,1)S(1)} %get-tuple-element.38), channel_id=1, source_target_pairs={{0,1},{1,0},{2,3},{3,2},{4,5},{5,4},{6,7},{7,6},{8,9},{9,8},{10,11... | collective-permute-start | bytes 589832 | tf_op jit(solution)/shard_map/ppermute | solution.py:532
  2.7 13.7 %collective-permute-start = (bf16[15,16,512]{2,1,0:T(8,128)(2,1)S(1)}, bf16[15,16,512]{2,1,0:T(8,128)(2,1)S(1)}, u32[]{:S(2)}, u32[]{:S(2)}) collective-permute-start(bf16[15,16,512]{2,1,0:T(8,128)(2,1)S(1)} %get-tuple-element.33), channel_id=1, source_target_pairs={{0,2},{4,6},{8,10},{12,14},{2,0},{6,4},{10,8},{14,12},{1,3},{5,7},... | collective-permute-start | bytes 737288 | tf_op jit(solution)/shard_map/ppermute | solution.py:524
  5.3 11.1 %collective-permute-start.1 = (bf16[15,16,512]{2,1,0:T(8,128)(2,1)S(1)}, bf16[15,16,512]{2,1,0:T(8,128)(2,1)S(1)}, u32[]{:S(2)}, u32[]{:S(2)}) collective-permute-start(bf16[15,16,512]{2,1,0:T(8,128)(2,1)S(1)} %get-tuple-element.34), channel_id=1, source_target_pairs={{2,4},{6,8},{10,12},{4,2},{8,6},{12,10},{3,5},{7,9},{11,13},{5,3},... | collective-permute-start | bytes 737288 | tf_op jit(solution)/shard_map/ppermute | solution.py:525
  16.5 2.1 %collective-permute-start.2 = (bf16[1,6,16,512]{3,2,1,0:T(8,128)(2,1)S(1)}, bf16[1,6,16,512]{3,2,1,0:T(8,128)(2,1)S(1)}, u32[]{:S(2)}, u32[]{:S(2)}) collective-permute-start(bf16[1,6,16,512]{3,2,1,0:T(8,128)(2,1)S(1)} %get-tuple-element.35), channel_id=1, source_target_pairs={{0,1},{1,0},{2,3},{3,2},{4,5},{5,4},{6,7},{7,6},{8,9},{9,8},{10,11... | collective-permute-start | bytes 294920 | tf_op jit(solution)/shard_map/ppermute | solution.py:532
